TPU v7x, 32 devices: a whole 2x2x4 slice. The times are simulated.
32 devices in a mesh: dp: 4 (over y, x), tensor: 2 (over core), expert: 4 (over z).
Axes of the slice: x: 2, y: 2, z: 4, core: 2. Of those that a mesh axis runs over, the one named last changes fastest.
Arguments:
- tokens: bfloat16 [2048, 2304], P(('dp', 'tensor', 'expert')), may hold values from -6 to 6
- routes: int32 [2048, 2], P(('dp', 'tensor', 'expert')), may hold values from 0 to 7, all different within a row; in each aligned block of 64 rows (0 to 63, 64 to 127, ...) at most 24 rows name the same one
- gates: float32 [2048, 2], P(('dp', 'tensor', 'expert')), may hold values from 0.2 to 1
- segments: int32 [2048], P(('dp', 'tensor', 'expert')), may hold values from 0 to 7, never falling along the last dimension, each value on 1 to 512 neighbouring positions
- w_gate: bfloat16 [8, 2304, 7680], P('expert', None, ('dp', 'tensor')), may hold values from -0.125 to 0.125
- w_up: bfloat16 [8, 2304, 7680], P('expert', None, ('dp', 'tensor')), may hold values from -0.125 to 0.125
- w_down: bfloat16 [8, 7680, 2304], P('expert', ('dp', 'tensor')), may hold values from -0.0625 to 0.0625
Outputs:
- embedded: bfloat16 [2048, 2304], P(('dp', 'tensor', 'expert'))
- pooled: float32 [8, 2304], replicated
Inputs may be any that keep to these rules, and one draw needn't show every extreme that they name: `routes`: each residue names two different experts. Within the rows of one device no expert is named more than 24 times, and in every draw some expert is named exactly 24 times by the rows of some device. `segments`: sequence numbers never fall along the residues; each sequence has 1 to 512 residues and one has exactly 512.
All inputs are finite; a program needn't handle non-finite values.
Results may differ from a plain program's by a relative error of at most 0.0085.
Values may be sent and summed in bfloat16 or wider, within the bound.
No kernel may reach another device: no remote copies, remote signals or barrier semaphores. Data moves between devices by JAX's collectives and lax.ppermute only.
A program may use at most 128 MiB of HBM per device.

v0:
```python
import jax
import jax.numpy as jnp
from jax import lax
from jax.sharding import PartitionSpec as P

EXPERTS = 8
TOP = 2
CAP = 24
epsilon = 1e-06


def norm_tokens(tokens):
    values = tokens.astype(jnp.float32)
    scale = lax.rsqrt(jnp.mean(values * values, axis=1, keepdims=True) + epsilon)
    return (values, (values * scale).astype(jnp.bfloat16))


def slot_numbers(routes):
    flat_routes = routes.reshape(-1)
    onehot = (flat_routes[:, None] == jnp.arange(EXPERTS, dtype=jnp.int32)[None, :]).astype(
        jnp.int32
    )
    before = jnp.cumsum(onehot, axis=0) - onehot
    slot_rank = jnp.sum(before * onehot, axis=1)
    return flat_routes * CAP + slot_rank


def placement_matrix(slot_index, tok_count):
    hits = (jnp.arange(EXPERTS * CAP, dtype=jnp.int32)[:, None] == slot_index[None, :]).astype(
        jnp.int32
    )
    return jnp.sum(hits.reshape(EXPERTS * CAP, tok_count, TOP), axis=2).astype(jnp.bfloat16)


def fan_out(slot_rows, replicas):
    leading = slot_rows.shape[:-2]
    features = slot_rows.shape[-1]
    shaped = slot_rows.reshape(leading + (EXPERTS, CAP, features))
    if replicas > 1:
        shaped = jnp.repeat(shaped, replicas, axis=len(leading))
    return shaped.reshape(leading + (EXPERTS * replicas * CAP, features))


def expert_hidden(row_block, w_gate, w_up):
    gate_proj = jnp.einsum("nacd,adf->nacf", row_block, w_gate, preferred_element_type=jnp.float32)
    up_proj = jnp.einsum("nacd,adf->nacf", row_block, w_up, preferred_element_type=jnp.float32)
    return (jax.nn.silu(gate_proj) * up_proj).astype(jnp.bfloat16)


def shards(tokens, routes, gates, segments, w_gate, w_up, w_down):
    tok_count = tokens.shape[0]
    width = tokens.shape[1]
    experts_axis = lax.axis_size("expert")
    per_device = w_gate.shape[0]
    replicas = max(1, experts_axis // EXPERTS)
    plane = lax.axis_size("dp") * lax.axis_size("tensor")
    values, normed = norm_tokens(tokens)
    slot_index = slot_numbers(routes)
    placing = placement_matrix(slot_index, tok_count)
    slot_rows = jnp.dot(placing, normed, preferred_element_type=jnp.float32).astype(jnp.bfloat16)
    send_rows = fan_out(slot_rows, replicas)
    received = lax.all_to_all(send_rows, "expert", split_axis=0, concat_axis=0, tiled=True)
    local_rows = received.reshape(experts_axis, per_device, CAP, width)
    hidden = expert_hidden(
        lax.all_gather(local_rows, ("dp", "tensor"), axis=0, tiled=True), w_gate, w_up
    )
    summed = lax.psum_scatter(
        jnp.einsum("nacf,afd->nacd", hidden, w_down, preferred_element_type=jnp.float32).astype(
            jnp.bfloat16
        ),
        ("dp", "tensor"),
        scatter_dimension=0,
        tiled=True,
    )
    returned = lax.all_to_all(summed, "expert", split_axis=0, concat_axis=0, tiled=True).astype(
        jnp.float32
    )
    if replicas > 1:
        expert_out = jnp.sum(returned.reshape(EXPERTS, replicas, CAP, width), axis=1)
    else:
        expert_out = returned.reshape(EXPERTS, CAP, width)
    picked = jnp.take(expert_out.reshape(EXPERTS * CAP, width), slot_index, axis=0).reshape(
        tok_count, TOP, width
    )
    mixed = values + jnp.sum(gates[:, :, None] * picked, axis=1)
    embedded = mixed.astype(jnp.bfloat16)
    devices_all = plane * experts_axis
    seq_total = tok_count * devices_all // 256
    seq_hot = (jnp.arange(seq_total, dtype=jnp.int32)[:, None] == segments[None, :]).astype(
        jnp.bfloat16
    )
    seq_sums = jnp.dot(seq_hot, embedded, preferred_element_type=jnp.float32)
    seq_counts = jnp.sum(seq_hot.astype(jnp.float32), axis=1)
    total_sums, total_counts = lax.psum((seq_sums, seq_counts), ("dp", "tensor", "expert"))
    pooled = total_sums / total_counts[:, None]
    return (embedded, pooled)


def solution(mesh):
    placed = (
        P(("dp", "tensor", "expert"), None),
        P(("dp", "tensor", "expert"), None),
        P(("dp", "tensor", "expert"), None),
        P(("dp", "tensor", "expert")),
        P("expert", None, ("dp", "tensor")),
        P("expert", None, ("dp", "tensor")),
        P("expert", ("dp", "tensor"), None),
    )
    return jax.shard_map(
        shards,
        mesh=mesh,
        in_specs=placed,
        out_specs=(P(("dp", "tensor", "expert"), None), P()),
        check_vma=False,
    )
```

profile of v0, /device:TPU:8, one launch (start us, length us, event | category | flops | bytes accessed | tf_op | source)
XLA Modules:
  0.0 401.1 jit_solution(3369024853161112235)
XLA Ops:
  7.2 0.8 copy.29
  8.0 0.1 reshape.84
  8.2 0.2 reduce_window_sum.11
  8.4 0.2 select_reduce_fusion
  8.6 0.1 reduce_sum.50
  8.8 0.7 compare_and_fusion
  9.6 1.1 fusion.14
  10.7 1.4 convolution_convert_fusion
  12.1 25.6 %all_to_all.14 = bf16[4,48,2304]{2,1,0:T(8,128)(2,1)S(1)} all-to-all(bf16[4,48,2304]{2,1,0:T(8,128)(2,1)S(1)} %bitcast.60), channel_id=1, replica_groups=mesh['dp'=4,'tensor'=2,'expert'=4] {'expert'}, dimensions={0} | all-to-all | bytes 1769472 | tf_op jit(solution)/shard_map/all_to_all | solution.py:62
  37.8 1.0 copy.32
  38.8 49.3 %all-gather.2.cloned.1.call-done = bf16[32,2,24,2304]{3,2,0,1:T(8,128)(2,1)} async-done(((bf16[4,2,24,2304]{3,2,0,1:T(8,128)(2,1)}), bf16[32,2,24,2304]{3,2,0,1:T(8,128)(2,1)}) %all-gather.2.cloned.1.call-update) | async-done | bytes 7077904 | tf_op jit(solution)/shard_map/all_gather | solution.py:65
  88.0 11.1 %fusion.2 = f32[2,32,24,960]{3,2,1,0:T(8,128)S(1)} fusion(bf16[32,2,24,2304]{3,2,0,1:T(8,128)(2,1)} %all-gather.2.cloned.1.call-done, bf16[2,2304,960]{1,2,0:T(8,128)(2,1)} %param.12), kind=kOutput, calls=%fused_computation.3 | convolution fusion | flops 6794772480 | bytes 21823488 | tf_op jit(solution)/shard_map/nacd,adf->nacf/dot_general | solution.py:46
  99.1 13.0 %fusion.8 = bf16[32,2,24,960]{3,2,0,1:T(8,128)(2,1)S(1)} fusion(f32[2,32,24,960]{3,2,1,0:T(8,128)S(1)} %fusion.2, bf16[32,2,24,2304]{3,2,0,1:T(8,128)(2,1)} %all-gather.2.cloned.1.call-done, bf16[2,2304,960]{1,2,0:T(8,128)(2,1)} %param.11), kind=kOutput, calls=%fused_computation.9 | convolution fusion | flops 6803619840 | bytes 24772608 | tf_op jit(solution)/shard_map/nacd,adf->nacf/dot_general | solution.py:45
  112.2 12.9 %convert_bitcast_fusion = bf16[32,2,24,2304]{3,2,0,1:T(8,128)(2,1)} fusion(bf16[32,2,24,960]{3,2,0,1:T(8,128)(2,1)S(1)} %fusion.8, bf16[2,960,2304]{2,1,0:T(8,128)(2,1)} %param.13), kind=kOutput, calls=%fused_computation.7 | convolution fusion | flops 6798311424 | bytes 18874368 | tf_op jit(solution)/shard_map/nacf,afd->nacd/dot_general | solution.py:68
  125.1 0.6 copy-done.5
  125.7 0.6 dynamic-slice
  126.9 111.2 %all-reduce.6.cloned.1.call-done = bf16[32,2,24,2304]{3,2,0,1:T(8,128)(2,1)} async-done(((bf16[32,2,24,2304]{3,2,0,1:T(8,128)(2,1)}), bf16[32,2,24,2304]{3,2,0,1:T(8,128)(2,1)}) %all-reduce.6.cloned.1.call-update) | async-done | bytes 7077904
  238.1 1.2 constant_dynamic-slice_fusion
  239.3 1.0 copy.33
  240.3 5.1 %all-to-all-start.1 = ((bf16[4,2,24,2304]{3,2,1,0:T(8,128)(2,1)}), bf16[4,2,24,2304]{3,2,1,0:T(8,128)(2,1)S(1)}, u32[]{:S(2)}, u32[]{:S(2)}) async-start(bf16[4,2,24,2304]{3,2,1,0:T(8,128)(2,1)} %copy.33), calls=%async_computation.1 | async-start | bytes 1769472 | tf_op jit(solution)/shard_map/all_to_all | solution.py:75
  245.5 0.1 mul.61
  245.7 0.1 copy.31
  245.9 18.3 %all-to-all-done.1 = bf16[4,2,24,2304]{3,2,1,0:T(8,128)(2,1)S(1)} async-done(((bf16[4,2,24,2304]{3,2,1,0:T(8,128)(2,1)}), bf16[4,2,24,2304]{3,2,1,0:T(8,128)(2,1)S(1)}, u32[]{:S(2)}, u32[]{:S(2)}) %all-to-all-start.1) | async-done | bytes 884768 | tf_op jit(solution)/shard_map/all_to_all | solution.py:75
  264.3 0.2 bitcast_convert_fusion
  264.5 1.1 gather_fusion
  265.5 0.7 gather.7
  266.2 3.2 multiply_reduce_fusion
  269.5 0.8 fusion.22
  270.3 0.1 convert_reduce_fusion.1
  270.5 41.4 %psum.15 = f32[8]{0:T(128)S(1)} all-reduce(f32[8]{0:T(128)S(1)} %convert_reduce_fusion.1), channel_id=1, replica_groups=mesh['dp'=4,'tensor'=2,'expert'=4] {'dp','tensor','expert'}, use_global_device_ids=true, to_apply=%region_8.9 | all-reduce | flops 8 | bytes 64 | tf_op jit(solution)/shard_map/psum | solution.py:94
  311.9 81.1 %all-reduce.4.cloned.1.call-done = f32[8,2304]{1,0:T(8,128)} async-done(((f32[8,2304]{1,0:T(8,128)}), f32[8,2304]{1,0:T(8,128)}) %all-reduce.4.cloned.1.call-update) | async-done | bytes 73744 | tf_op jit(solution)/shard_map/psum | solution.py:94
  393.0 1.6 broadcast_divide_fusion
  (27 shorter events, 0.7 us)
Async XLA Ops:
  7.2 80.9 %all-gather.2.cloned.1.call-start = ((), (), s32[]{:S(2)}) async-start(), calls=%async_computation.2 | async-start | bytes 7962624 | tf_op jit(solution)/shard_map/all_gather | solution.py:65
  38.7 199.4 %all-reduce.6.cloned.1.call-start = ((), (), s32[]{:S(2)}) async-start(), calls=%async_computation.4 | async-start | bytes 14155776
  125.0 0.7 copy-start.5
  125.0 120.4 %copy-start.2 = (s32[64,2]{0,1:T(2,128)S(1)}, s32[64,2]{0,1:T(2,128)}, u32[]{:S(2)}) copy-start(s32[64,2]{0,1:T(2,128)} %param.8) | copy-start | bytes 1540
  125.0 120.8 %copy-start.3 = (f32[64,2]{0,1:T(2,128)S(1)}, f32[64,2]{0,1:T(2,128)}, u32[]{:S(2)}) copy-start(f32[64,2]{0,1:T(2,128)} %param.9) | copy-start | bytes 1540
  240.3 24.0 %all-to-all-start.1 = ((bf16[4,2,24,2304]{3,2,1,0:T(8,128)(2,1)}), bf16[4,2,24,2304]{3,2,1,0:T(8,128)(2,1)S(1)}, u32[]{:S(2)}, u32[]{:S(2)}) async-start(bf16[4,2,24,2304]{3,2,1,0:T(8,128)(2,1)} %copy.33), calls=%async_computation.1 | async-start | bytes 1769472 | tf_op jit(solution)/shard_map/all_to_all | solution.py:75
  245.4 147.5 %all-reduce.4.cloned.1.call-start = ((), (), s32[]{:S(2)}) async-start(), calls=%async_computation.3 | async-start | bytes 147456 | tf_op jit(solution)/shard_map/psum | solution.py:94
  264.4 5.0 %copy-start = (bf16[64,2304]{1,0:T(8,128)(2,1)S(1)}, bf16[64,2304]{1,0:T(8,128)(2,1)}, u32[]{:S(2)}) copy-start(bf16[64,2304]{1,0:T(8,128)(2,1)} %param.7) | copy-start | bytes 884740
  264.4 5.1 %copy-start.4 = (s32[64]{0:T(128)S(1)}, s32[64]{0:T(128)}, u32[]{:S(2)}) copy-start(s32[64]{0:T(128)} %param.10) | copy-start | bytes 772
  269.5 125.1 %copy-start.1 = (bf16[64,2304]{1,0:T(8,128)(2,1)}, bf16[64,2304]{1,0:T(8,128)(2,1)S(1)}, u32[]{:S(2)}) copy-start(bf16[64,2304]{1,0:T(8,128)(2,1)S(1)} %fusion.16) | copy-start | bytes 884740
Sparse Core Ops, SparseCore 0:
  38.9 49.1 all-gather.1
  125.2 112.8 all-reduce.5
  270.5 122.4 all-reduce.3
where the time goes:
time: 402 us; the launch traced here: 401 us
  waiting for transfers between devices  260 us (65%)
  blocking collectives  67 us (17%)
  matrix products  39.2 us (10%)
  between operations  14.6 us (4%)
  local copies, waits for them, and re-layouts  7.73 us (2%)
  other arithmetic  7.49 us (2%)
  starting transfers between devices  5.22 us (1%)
    unnamed x4, waiting for transfers between devices  111 us
    psum x1, waiting for transfers between devices, shards(): lax.psum((seq_sums, seq_counts), ('dp', 'tensor', 'expert'))  81.1 us
    all_gather x1, waiting for transfers between devices, shards(): lax.all_gather(local_rows, ('dp', 'tensor'), axis=0, tiled=True)  49.3 us
    psum x1, blocking collectives, shards(): lax.psum((seq_sums, seq_counts), ('dp', 'tensor', 'expert'))  41.4 us
    all_to_all x1, blocking collectives, shards(): lax.all_to_all(send_rows, 'expert', split_axis=0, concat_axis=0, tiled=True)  25.6 us
    all_to_all x1, waiting for transfers between devices, shards(): lax.all_to_all(summed, 'expert', split_axis=0, concat_axis=0, tiled=True)  18.3 us
    dot_general x1, matrix products, expert_hidden(): jnp.einsum('nacd,adf->nacf', row_block, w_gate, preferred_element_type=jn...  13 us
    dot_general x1, matrix products, shards(): jnp.einsum('nacf,afd->nacd', hidden, w_down, preferred_element_type=jnp.f...  12.9 us
  transfers between devices with their start and end apart: 4, of which 4 were waited for; matrix products, arithmetic and copies ran while one was open for 0% of the time, Pallas kernels for 0%

commit v1 on v0

--- a/solution.py
+++ b/solution.py
@@ -7,6 +7,11 @@
 TOP = 2
 CAP = 24
 epsilon = 1e-06
+
+
+def one_after_other(x, inner_axis, outer_axis):
+    half = lax.psum(x, inner_axis)
+    return lax.psum(half, outer_axis)
 
 
 def norm_tokens(tokens):
@@ -91,7 +96,7 @@
     )
     seq_sums = jnp.dot(seq_hot, embedded, preferred_element_type=jnp.float32)
     seq_counts = jnp.sum(seq_hot.astype(jnp.float32), axis=1)
-    total_sums, total_counts = lax.psum((seq_sums, seq_counts), ("dp", "tensor", "expert"))
+    total_sums, total_counts = one_after_other((seq_sums, seq_counts), ("tensor", "expert"), "dp")
     pooled = total_sums / total_counts[:, None]
     return (embedded, pooled)
 

time: 402 us -> 377 us (0.938)
  blocking collectives: 67 us -> 48.5 us
  waiting for transfers between devices: 260 us -> 252 us
    psum x1 -> x2, blocking collectives: 41.4 us -> 22.9 us  [the longest x1 13.1 us: one_after_other(): half = lax.psum(x, inner_axis)]
    psum x1 -> x2, waiting for transfers between devices: 81.1 us -> 73.6 us  [the longest x1 53.2 us: one_after_other(): half = lax.psum(x, inner_axis)]
    unnamed x4 -> x5, waiting for transfers between devices: 111 us -> 111 us
  transfers between devices with their start and end apart: 4 -> 5, of which waited for: 4 -> 5; matrix products, arithmetic and copies ran while one was open for 0% -> 0% of each run, Pallas kernels for 0% -> 0%
where the time goes in v1:
time: 377 us; the launch traced here: 375 us
  waiting for transfers between devices  252 us (67%)
  blocking collectives  48.5 us (13%)
  matrix products  39.2 us (10%)
  between operations  14.6 us (4%)
  local copies, waits for them, and re-layouts  7.73 us (2%)
  other arithmetic  7.49 us (2%)
  starting transfers between devices  5.26 us (1%)
    unnamed x5, waiting for transfers between devices  111 us
    psum x1, waiting for transfers between devices, one_after_other(): half = lax.psum(x, inner_axis)  53.2 us
    all_gather x1, waiting for transfers between devices, shards(): lax.all_gather(local_rows, ('dp', 'tensor'), axis=0, tiled=True)  49.3 us
    all_to_all x1, blocking collectives, shards(): lax.all_to_all(send_rows, 'expert', split_axis=0, concat_axis=0, tiled=True)  25.6 us
    psum x1, waiting for transfers between devices, one_after_other(): return lax.psum(half, outer_axis)  20.4 us
    all_to_all x1, waiting for transfers between devices, shards(): lax.all_to_all(summed, 'expert', split_axis=0, concat_axis=0, tiled=True)  18.3 us
    psum x1, blocking collectives, one_after_other(): half = lax.psum(x, inner_axis)  13.1 us
    dot_general x1, matrix products, expert_hidden(): jnp.einsum('nacd,adf->nacf', row_block, w_gate, preferred_element_type=jn...  13 us
  transfers between devices with their start and end apart: 5, of which 5 were waited for; matrix products, arithmetic and copies ran while one was open for 0% of the time, Pallas kernels for 0%

profile of v1, /device:TPU:8, one launch (start us, length us, event | category | flops | bytes accessed | tf_op | source)
XLA Modules:
  0.0 375.1 jit_solution(13139870784524885286)
XLA Ops:
  7.2 0.8 copy.29
  8.0 0.1 reshape.84
  8.2 0.2 reduce_window_sum.11
  8.4 0.2 select_reduce_fusion
  8.6 0.1 reduce_sum.50
  8.8 0.7 compare_and_fusion
  9.6 1.1 fusion.14
  10.7 1.4 convolution_convert_fusion
  12.1 25.6 %all_to_all.14 = bf16[4,48,2304]{2,1,0:T(8,128)(2,1)S(1)} all-to-all(bf16[4,48,2304]{2,1,0:T(8,128)(2,1)S(1)} %bitcast.60), channel_id=1, replica_groups=mesh['dp'=4,'tensor'=2,'expert'=4] {'expert'}, dimensions={0} | all-to-all | bytes 1769472 | tf_op jit(solution)/shard_map/all_to_all | solution.py:67
  37.8 1.0 copy.32
  38.8 49.3 %all-gather.2.cloned.1.call-done = bf16[32,2,24,2304]{3,2,0,1:T(8,128)(2,1)} async-done(((bf16[4,2,24,2304]{3,2,0,1:T(8,128)(2,1)}), bf16[32,2,24,2304]{3,2,0,1:T(8,128)(2,1)}) %all-gather.2.cloned.1.call-update) | async-done | bytes 7077904 | tf_op jit(solution)/shard_map/all_gather | solution.py:70
  88.0 11.1 %fusion.2 = f32[2,32,24,960]{3,2,1,0:T(8,128)S(1)} fusion(bf16[32,2,24,2304]{3,2,0,1:T(8,128)(2,1)} %all-gather.2.cloned.1.call-done, bf16[2,2304,960]{1,2,0:T(8,128)(2,1)} %param.12), kind=kOutput, calls=%fused_computation.3 | convolution fusion | flops 6794772480 | bytes 21823488 | tf_op jit(solution)/shard_map/nacd,adf->nacf/dot_general | solution.py:51
  99.1 13.0 %fusion.8 = bf16[32,2,24,960]{3,2,0,1:T(8,128)(2,1)S(1)} fusion(f32[2,32,24,960]{3,2,1,0:T(8,128)S(1)} %fusion.2, bf16[32,2,24,2304]{3,2,0,1:T(8,128)(2,1)} %all-gather.2.cloned.1.call-done, bf16[2,2304,960]{1,2,0:T(8,128)(2,1)} %param.11), kind=kOutput, calls=%fused_computation.9 | convolution fusion | flops 6803619840 | bytes 24772608 | tf_op jit(solution)/shard_map/nacd,adf->nacf/dot_general | solution.py:50
  112.2 12.9 %convert_bitcast_fusion = bf16[32,2,24,2304]{3,2,0,1:T(8,128)(2,1)} fusion(bf16[32,2,24,960]{3,2,0,1:T(8,128)(2,1)S(1)} %fusion.8, bf16[2,960,2304]{2,1,0:T(8,128)(2,1)} %param.13), kind=kOutput, calls=%fused_computation.7 | convolution fusion | flops 6798311424 | bytes 18874368 | tf_op jit(solution)/shard_map/nacf,afd->nacd/dot_general | solution.py:73
  125.1 0.6 copy-done.5
  125.7 0.6 dynamic-slice
  126.9 111.2 %all-reduce.9.cloned.1.call-done = bf16[32,2,24,2304]{3,2,0,1:T(8,128)(2,1)} async-done(((bf16[32,2,24,2304]{3,2,0,1:T(8,128)(2,1)}), bf16[32,2,24,2304]{3,2,0,1:T(8,128)(2,1)}) %all-reduce.9.cloned.1.call-update) | async-done | bytes 7077904
  238.1 1.2 constant_dynamic-slice_fusion
  239.3 1.0 copy.33
  240.3 5.1 %all-to-all-start.1 = ((bf16[4,2,24,2304]{3,2,1,0:T(8,128)(2,1)}), bf16[4,2,24,2304]{3,2,1,0:T(8,128)(2,1)S(1)}, u32[]{:S(2)}, u32[]{:S(2)}) async-start(bf16[4,2,24,2304]{3,2,1,0:T(8,128)(2,1)} %copy.33), calls=%async_computation.1 | async-start | bytes 1769472 | tf_op jit(solution)/shard_map/all_to_all | solution.py:80
  245.5 0.1 mul.61
  245.9 18.3 %all-to-all-done.1 = bf16[4,2,24,2304]{3,2,1,0:T(8,128)(2,1)S(1)} async-done(((bf16[4,2,24,2304]{3,2,1,0:T(8,128)(2,1)}), bf16[4,2,24,2304]{3,2,1,0:T(8,128)(2,1)S(1)}, u32[]{:S(2)}, u32[]{:S(2)}) %all-to-all-start.1) | async-done | bytes 884768 | tf_op jit(solution)/shard_map/all_to_all | solution.py:80
  264.3 0.2 bitcast_convert_fusion
  264.5 1.1 gather_fusion
  265.5 0.7 gather.7
  266.2 3.2 multiply_reduce_fusion
  269.5 0.8 fusion.22
  270.4 53.2 %all-reduce.5.cloned.1.call-done = f32[8,2304]{1,0:T(8,128)} async-done(((f32[8,2304]{1,0:T(8,128)}), f32[8,2304]{1,0:T(8,128)}) %all-reduce.5.cloned.1.call-update) | async-done | bytes 73744 | tf_op jit(solution)/shard_map/psum | solution.py:13
  323.7 13.1 %psum.30 = f32[8]{0:T(128)S(1)} all-reduce(f32[8]{0:T(128)S(1)} %convert_reduce_fusion.1), channel_id=1, replica_groups=mesh['dp'=4,'tensor'=2,'expert'=4] {'tensor','expert'}, use_global_device_ids=true, to_apply=%region_9.10 | all-reduce | flops 8 | bytes 64 | tf_op jit(solution)/shard_map/psum | solution.py:13
  336.8 9.8 %psum.31 = f32[8]{0:T(128)S(1)} all-reduce(f32[8]{0:T(128)S(1)} %psum.30), channel_id=1, replica_groups=mesh['dp'=4,'tensor'=2,'expert'=4] {'dp'}, use_global_device_ids=true, to_apply=%region_10.11 | all-reduce | flops 8 | bytes 64 | tf_op jit(solution)/shard_map/psum | solution.py:14
  346.6 20.4 %all-reduce.7.cloned.1.call-done = f32[8,2304]{1,0:T(8,128)} async-done(((f32[8,2304]{1,0:T(8,128)}), f32[8,2304]{1,0:T(8,128)}) %all-reduce.7.cloned.1.call-update) | async-done | bytes 73744 | tf_op jit(solution)/shard_map/psum | solution.py:14
  367.0 1.6 broadcast_divide_fusion
  (31 shorter events, 1.0 us)
Async XLA Ops:
  7.2 80.9 %all-gather.2.cloned.1.call-start = ((), (), s32[]{:S(2)}) async-start(), calls=%async_computation.2 | async-start | bytes 7962624 | tf_op jit(solution)/shard_map/all_gather | solution.py:70
  38.7 199.4 %all-reduce.9.cloned.1.call-start = ((), (), s32[]{:S(2)}) async-start(), calls=%async_computation.5 | async-start | bytes 14155776
  125.0 0.7 copy-start.5
  125.0 120.4 %copy-start.2 = (s32[64,2]{0,1:T(2,128)S(1)}, s32[64,2]{0,1:T(2,128)}, u32[]{:S(2)}) copy-start(s32[64,2]{0,1:T(2,128)} %param.8) | copy-start | bytes 1540
  125.0 120.8 %copy-start.3 = (f32[64,2]{0,1:T(2,128)S(1)}, f32[64,2]{0,1:T(2,128)}, u32[]{:S(2)}) copy-start(f32[64,2]{0,1:T(2,128)} %param.9) | copy-start | bytes 1540
  240.3 24.0 %all-to-all-start.1 = ((bf16[4,2,24,2304]{3,2,1,0:T(8,128)(2,1)}), bf16[4,2,24,2304]{3,2,1,0:T(8,128)(2,1)S(1)}, u32[]{:S(2)}, u32[]{:S(2)}) async-start(bf16[4,2,24,2304]{3,2,1,0:T(8,128)(2,1)} %copy.33), calls=%async_computation.1 | async-start | bytes 1769472 | tf_op jit(solution)/shard_map/all_to_all | solution.py:80
  245.4 78.1 %all-reduce.5.cloned.1.call-start = ((), (), s32[]{:S(2)}) async-start(), calls=%async_computation.3 | async-start | bytes 147456 | tf_op jit(solution)/shard_map/psum | solution.py:13
  264.4 5.0 %copy-start = (bf16[64,2304]{1,0:T(8,128)(2,1)S(1)}, bf16[64,2304]{1,0:T(8,128)(2,1)}, u32[]{:S(2)}) copy-start(bf16[64,2304]{1,0:T(8,128)(2,1)} %param.7) | copy-start | bytes 884740
  264.4 5.1 %copy-start.4 = (s32[64]{0:T(128)S(1)}, s32[64]{0:T(128)}, u32[]{:S(2)}) copy-start(s32[64]{0:T(128)} %param.10) | copy-start | bytes 772
  269.5 99.1 %copy-start.1 = (bf16[64,2304]{1,0:T(8,128)(2,1)}, bf16[64,2304]{1,0:T(8,128)(2,1)S(1)}, u32[]{:S(2)}) copy-start(bf16[64,2304]{1,0:T(8,128)(2,1)S(1)} %fusion.16) | copy-start | bytes 884740
  270.3 96.7 %all-reduce.7.cloned.1.call-start = ((), (), s32[]{:S(2)}) async-start(), calls=%async_computation.4 | async-start | bytes 147456 | tf_op jit(solution)/shard_map/psum | solution.py:14
Sparse Core Ops, SparseCore 0:
  38.9 49.1 all-gather.1
  125.2 112.8 all-reduce.8
  270.5 53.0 all-reduce.4
  326.6 40.3 all-reduce.6
